TPU v7x, 512 devices: a whole 4x8x8 slice. The times are simulated.
512 devices in a mesh: seq: 16 (over z, core), dp: 8 (over y), mp: 4 (over x).
Axes of the slice: x: 4, y: 8, z: 8, core: 2. Of those that a mesh axis runs over, the one named last changes fastest.
Arguments:
- features: bfloat16 [8, 4096, 8, 512], P('dp', 'seq', None, 'mp'), may hold values from -6 to 6
- key_projection: bfloat16 [8, 4096, 8, 128], P('dp', 'seq'), may hold values from -2 to 2
- query_proj: bfloat16 [8, 4096, 8, 128], P('dp', 'seq'), may hold values from -2 to 2
- step_raw: float32 [8, 4096, 8, 8], P('dp', 'seq', None, 'mp'), may hold values from -3 to 6
- doc_starts: int32 [8, 4096], P('dp', 'seq'), may hold values 0 or 1
- log_rate: float32 [8, 8], P(None, 'mp'), may hold values from -5 to 1
- step_bias: float32 [8, 8], P(None, 'mp'), may hold values from -5 to -2.5
- skip_gain: float32 [8, 8], P(None, 'mp'), may hold values from 0.5 to 1.5
- out_grad: bfloat16 [8, 4096, 8, 512], P('dp', 'seq', None, 'mp'), may hold values from -6 to 6
Outputs:
- mixed_out: bfloat16 [8, 4096, 8, 512], P('dp', 'seq', None, 'mp')
- features_grad: bfloat16 [8, 4096, 8, 512], P('dp', 'seq', None, 'mp')
- key_grad: bfloat16 [8, 4096, 8, 128], P('dp', 'seq', 'mp')
- query_grad: bfloat16 [8, 4096, 8, 128], P('dp', 'seq', 'mp')
- step_grad: float32 [8, 4096, 8, 8], P('dp', 'seq', None, 'mp')
- log_rate_grad: float32 [8, 8], P(None, 'mp')
- step_bias_grad: float32 [8, 8], P(None, 'mp')
- skip_grad: float32 [8, 8], P(None, 'mp')
All inputs are finite; a program needn't handle non-finite values. No bound on the sum of `doc_starts` on one device may be relied on, other than what follows from the above.
Results may differ from a plain program's by a relative error of at most 0.0015.
Values sent between devices are 32-bit elements; how exact they have to be, the bound alone decides.
No kernel may reach another device: no remote copies, remote signals or barrier semaphores. Data moves between devices by JAX's collectives and lax.ppermute only.
A program may use at most 128 MiB of HBM per device.

v0:
```python
import math
import jax
import jax.numpy as jnp
from jax import lax
from jax.sharding import PartitionSpec as P

P_SIZE = 64
triple = lax.Precision.HIGH


def prefix(shard, axis, combine, identity, reverse):
    length, position = (lax.axis_size(axis), lax.axis_index(axis))
    everything = jax.tree.map(lambda part: lax.all_gather(part, axis), shard)
    start = jax.tree.map(
        lambda part, zero: jnp.broadcast_to(jnp.asarray(zero, part.dtype), part.shape),
        shard,
        identity,
    )

    def step(k, before):
        at = length - 1 - k if reverse else k
        reached = at > position if reverse else at < position
        new = combine(before, jax.tree.map(lambda part: part[at], everything))
        return jax.tree.map(lambda a, b: jnp.where(reached, a, b), new, before)

    return lax.fori_loop(0, length, step, start)


def decay_terms(step_raw, doc_starts, log_rate, step_bias):
    step_size = jax.nn.softplus(step_raw + step_bias)
    log_decay = -step_size * jnp.exp(log_rate)
    cumulative = jnp.cumsum(log_decay, axis=1)
    doc_count = jnp.cumsum(doc_starts, axis=1)
    return (step_size, cumulative, doc_count)


def block_forward(
    head_vals, key_vals, query_vals, step_raw, doc_starts, log_rate, step_bias, skip_gain, state_in
):
    step_size, cumulative, doc_count = decay_terms(step_raw, doc_starts, log_rate, step_bias)
    block_len = head_vals.shape[1]
    causal = jnp.arange(block_len)[:, None] >= jnp.arange(block_len)[None, :]
    same_doc = causal[None] & (doc_count[:, :, None] == doc_count[:, None, :])
    doc_mask = same_doc[..., None, None]
    gap_log = cumulative[:, :, None] - cumulative[:, None, :]
    decay_mat = jnp.where(doc_mask, jnp.exp(jnp.where(doc_mask, gap_log, 0.0)), 0.0)
    entry_decay = jnp.where((doc_count == 0)[:, :, None, None], jnp.exp(cumulative), 0.0)
    scores = jnp.einsum("rtgn,rsgn->rtsg", query_vals, key_vals, precision=triple)
    mixing = scores[..., None] * decay_mat * step_size[:, None]
    output = jnp.einsum("rtsgh,rsghp->rtghp", mixing, head_vals, precision=triple)
    output = (
        output
        + jnp.einsum("rtgn,rghpn->rtghp", query_vals, state_in, precision=triple)
        * entry_decay[..., None]
    )
    output = output + skip_gain[..., None] * head_vals
    last_decay = decay_mat[:, -1]
    state_out = state_in * entry_decay[:, -1][..., None, None]
    state_out = state_out + jnp.einsum(
        "rsgh,rsghp,rsgn->rghpn", last_decay * step_size, head_vals, key_vals, precision=triple
    )
    return (output, state_out)


def block_summary(head_vals, key_vals, step_raw, doc_starts, log_rate, step_bias):
    step_size, cumulative, doc_count = decay_terms(step_raw, doc_starts, log_rate, step_bias)
    tail_doc = (doc_count == doc_count[:, -1:])[:, :, None, None]
    last_decay = jnp.where(
        tail_doc, jnp.exp(jnp.where(tail_doc, cumulative[:, -1:] - cumulative, 0.0)), 0.0
    )
    passed_forward = jnp.where(
        (doc_count[:, -1] == 0)[:, None, None], jnp.exp(cumulative[:, -1]), 0.0
    )
    summary_state = jnp.einsum(
        "rsgh,rsghp,rsgn->rghpn", last_decay * step_size, head_vals, key_vals, precision=triple
    )
    return (passed_forward, summary_state)


def forward_combine(earlier, trailing_portion):
    return (
        earlier[0] * trailing_portion[0],
        trailing_portion[0][..., None, None] * earlier[1] + trailing_portion[1],
    )


def backward_combine(earlier, trailing_portion):
    return (
        earlier[0] * trailing_portion[0],
        trailing_portion[1] + trailing_portion[0][..., None, None] * earlier[1],
    )


def local(
    features,
    key_projection,
    query_proj,
    step_raw,
    doc_starts,
    log_rate,
    step_bias,
    skip_gain,
    out_grad,
):
    row_count, length, groups, feat_width = features.shape
    head_count = feat_width // P_SIZE
    block_len = math.gcd(length, 128)
    block_count = length // block_len
    head_vals = features.astype(jnp.float32).reshape(row_count, length, groups, head_count, P_SIZE)
    key_vals = key_projection.astype(jnp.float32)
    query_vals = query_proj.astype(jnp.float32)
    passed_forward, summary_state = block_summary(
        head_vals, key_vals, step_raw, doc_starts, log_rate, step_bias
    )
    state_in = prefix(
        (passed_forward, summary_state),
        "seq",
        forward_combine,
        (jnp.ones_like(passed_forward), jnp.zeros_like(summary_state)),
        False,
    )[1]

    def to_blocks(array):
        return jnp.moveaxis(
            array.reshape((row_count, block_count, block_len) + array.shape[2:]), 1, 0
        )

    def local_layer(
        head_vals, key_vals, query_vals, step_raw, log_rate, step_bias, skip_gain, state_in
    ):

        def stepper(state, pieces):
            vals_b, keys_b, queries_b, raw_b, starts_b = pieces
            output, new_state = block_forward(
                vals_b, keys_b, queries_b, raw_b, starts_b, log_rate, step_bias, skip_gain, state
            )
            return (new_state, output)

        final_state, block_outs = lax.scan(
            jax.checkpoint(stepper),
            state_in,
            (
                to_blocks(head_vals),
                to_blocks(key_vals),
                to_blocks(query_vals),
                to_blocks(step_raw),
                to_blocks(doc_starts),
            ),
        )
        outputs = jnp.moveaxis(block_outs, 0, 1).reshape(
            row_count, length, groups, head_count, P_SIZE
        )
        return (outputs, final_state)

    primal, pullback = jax.vjp(
        local_layer,
        head_vals,
        key_vals,
        query_vals,
        step_raw,
        log_rate,
        step_bias,
        skip_gain,
        state_in,
    )
    mixed_vals = primal[0]
    cotangent = out_grad.astype(jnp.float32).reshape(head_vals.shape)
    _, cumulative, doc_count = decay_terms(step_raw, doc_starts, log_rate, step_bias)
    entry_decay = jnp.where((doc_count == 0)[:, :, None, None], jnp.exp(cumulative), 0.0)
    adjoint_local = jnp.einsum(
        "rtgh,rtghp,rtgn->rghpn", entry_decay, cotangent, query_vals, precision=triple
    )
    adjoint_in = prefix(
        (passed_forward, adjoint_local),
        "seq",
        backward_combine,
        (jnp.ones_like(passed_forward), jnp.zeros_like(adjoint_local)),
        True,
    )[1]
    gradients = pullback((cotangent, adjoint_in))
    vals_grad, keys_grad, queries_grad, raw_grad, rate_grad, bias_grad, gain_grad, _ = gradients
    key_part, query_part = (
        lax.psum_scatter(keys_grad, "mp", scatter_dimension=2, tiled=True),
        lax.psum_scatter(queries_grad, "mp", scatter_dimension=2, tiled=True),
    )
    rate_total, bias_total, gain_total = lax.psum((rate_grad, bias_grad, gain_grad), ("seq", "dp"))
    return (
        mixed_vals.reshape(features.shape).astype(jnp.bfloat16),
        vals_grad.reshape(features.shape).astype(jnp.bfloat16),
        key_part.astype(jnp.bfloat16),
        query_part.astype(jnp.bfloat16),
        raw_grad,
        rate_total,
        bias_total,
        gain_total,
    )


def solution(mesh):
    return jax.shard_map(
        local,
        mesh=mesh,
        in_specs=(
            P("dp", "seq", None, "mp"),
            P("dp", "seq", None, None),
            P("dp", "seq", None, None),
            P("dp", "seq", None, "mp"),
            P("dp", "seq"),
            P(None, "mp"),
            P(None, "mp"),
            P(None, "mp"),
            P("dp", "seq", None, "mp"),
        ),
        out_specs=(
            P("dp", "seq", None, "mp"),
            P("dp", "seq", None, "mp"),
            P("dp", "seq", "mp", None),
            P("dp", "seq", "mp", None),
            P("dp", "seq", None, "mp"),
            P(None, "mp"),
            P(None, "mp"),
            P(None, "mp"),
        ),
        check_vma=False,
    )
```

profile of v0, /device:TPU:2, one launch (start us, length us, event | category | flops | bytes accessed | tf_op | source)
XLA Modules:
  0.0 560.6 jit_solution(17976242943628089828)
XLA Ops:
  14.2 1.3 copy.473
  15.7 2.3 fusion.127
  19.0 1.3 copy.464
  21.8 1.5 reshape.1086
  24.7 2.1 copy.470
  26.8 2.1 copy.469
  30.1 23.6 %all_gather.18 = f32[16,1,8,2]{2,3,1,0:T(2,128)S(1)} all-gather(f32[1,1,8,2]{2,3,1,0:T(2,128)S(1)} %copy.462), channel_id=1, replica_groups=mesh['seq'=16,'dp'=8,'mp'=4] {'seq'}, dimensions={0}, use_global_device_ids=true | all-gather | bytes 1088 | tf_op jit(solution)/shard_map/all_gather | solution.py:13
  53.7 28.4 %all-gather.7.cloned.1.call-done = f32[128,2,64,128]{3,2,1,0:T(8,128)} async-done(((f32[8,2,64,128]{3,2,1,0:T(8,128)}), f32[128,2,64,128]{3,2,1,0:T(8,128)}) %all-gather.7.cloned.1.call-update) | async-done | bytes 8388624 | tf_op jit(solution)/shard_map/all_gather | solution.py:13
  82.1 20.8 %while.78 = (s32[]{:T(128)}, f32[1,8,2,64,128]{4,3,2,1,0:T(8,128)S(1)}, s32[]{:T(128)}, f32[16,1,8,2,64,128]{5,4,3,2,1,0:T(8,128)}, f32[16,1,8,2]{2,3,1,0:T(2,12...) while((s32[]{:T(128)}, f32[1,8,2,64,128]{4,3,2,1,0:T(8,128)S(1)}, s32[]{:T(128)}, ...), condition=%wide.region_11.12_spmd.clone, body=%wide.region_10.11_spmd.clone.sunk | while | flops 524296 | bytes 1573359 | solution.py:26
  102.9 39.2 %all-gather.5.cloned.1.call-done = f32[128,2,64,128]{3,2,1,0:T(8,128)} async-done(((f32[8,2,64,128]{3,2,1,0:T(8,128)}), f32[128,2,64,128]{3,2,1,0:T(8,128)}) %all-gather.5.cloned.1.call-update) | async-done | bytes 8388624 | tf_op jit(solution)/shard_map/all_gather | solution.py:13
  142.1 20.6 %while.77 = (s32[]{:T(128)}, f32[1,8,2,64,128]{4,3,2,1,0:T(8,128)S(1)}, s32[]{:T(128)}, f32[16,1,8,2]{2,3,1,0:T(2,128)S(1)}, f32[16,1,8,2,64,128]{5,4,3,2,1,0:T(8,128)}, /*index=5*/s32[]{:T(128)}, s32[]{:T(128)}) while((s32[]{:T(128)}, f32[1,8,2,64,128]{4,3,2,1,0:T(8,128)S(1)}, s32[]{:T(128)}, f32[16,1,8,2]{2,3,1,0:T(2,128)S(1)}, ...), condition=%wide.region_5.6_spmd.clone, body=%wide.region_4.5_spmd.clone.sunk | while | flops 524292 | bytes 1573297 | solution.py:26
  163.7 30.4 %while.76 = (s32[]{:T(128)}, f32[1,8,2,64,128]{4,3,2,1,0:T(8,128)S(1)}, bf16[2,1,128,8,2,64]{2,5,4,3,1,0:T(8,128)(2,1)}, f32[2,1,8,2,64,128]{5,4,3,2,1,0:T(8,128...) while((s32[]{:T(128)}, ...), condition=%wide.region_9.10_spmd.clone, body=%wide.region_6.9_spmd.clone.sunk | while | flops 405264384 | bytes 14427908 | solution.py:139
  168.5 1.8 fusion.210
  170.3 1.9 convolution_bitcast_fusion.16
  173.2 3.3 fusion.211
  177.3 1.5 fusion.209
  183.7 1.8 fusion.210
  185.5 1.9 convolution_bitcast_fusion.16
  188.4 3.3 fusion.211
  192.5 1.5 fusion.209
  197.8 90.8 %while.79 = (s32[]{:T(128)}, f32[8,2]{1,0:T(8,128)}, f32[8,2]{0,1:T(2,128)}, f32[8,2]{1,0:T(8,128)}, f32[1,8,2,64,128]{4,3,2,1,0:T(8,128)S(1)}, /*index=5*/bf16[...) while((s32[]{:T(128)}, f32[8,2]{1,0:T(8,128)}, ...), condition=%wide.region_25.26_spmd.clone, body=%wide.region_12.25_spmd.clone.sunk | while | flops 1015154816 | bytes 36794436 | solution.py:139
  198.5 1.8 constant_dynamic-slice_fusion.4
  202.4 1.5 dynamic-slice_bitcast_fusion.19
  207.4 1.5 convolution_bitcast_fusion.17
  208.9 2.0 copy.623
  210.9 2.0 copy.612
  212.9 1.5 fusion.234
  220.5 1.6 convolution_bitcast_fusion.19
  223.2 3.3 fusion.239
  229.7 1.9 fusion.242
  235.7 2.7 fusion.245
  238.4 1.4 dynamic_update_slice.74
  243.2 1.8 constant_dynamic-slice_fusion.4
  247.2 1.5 dynamic-slice_bitcast_fusion.19
  249.8 1.3 select_add_fusion.8
  252.8 1.5 convolution_bitcast_fusion.17
  254.3 2.0 copy.623
  256.3 2.0 copy.612
  258.4 1.5 fusion.234
  265.9 1.6 convolution_bitcast_fusion.19
  268.6 3.3 fusion.239
  275.1 1.9 fusion.242
  281.7 2.7 fusion.245
  284.5 1.4 dynamic_update_slice.74
  290.7 250.9 %all-reduce.2 = (f32[8,2]{0,1:T(2,128)}, f32[8,2]{0,1:T(2,128)}, f32[8,2]{0,1:T(2,128)}) all-reduce(f32[8,2]{0,1:T(2,128)} %get-tuple-element.780, f32[8,2]{0,1:T(2,128)S(1)} %copy.487, f32[8,2]{0,1:T(2,128)S(1)} %copy.488), channel_id=1, replica_groups=mesh['seq'=16,'dp'=8,'mp'=4] {'seq','dp'}, use_global_device_ids=true, to_apply=%region_28.29 | all-reduce | flops 48 | bytes 384 | tf_op jit(solution)/shard_map/psum | solution.py:186
  541.7 1.3 transpose.190
  543.0 2.5 copy.509
  546.8 2.5 copy.512
  (310 shorter events, 124.0 us)
Async XLA Ops:
  7.2 14.6 %copy-start.4 = (f32[1,256,8,2]{1,3,2,0:T(2,128)S(1)}, f32[1,256,8,2]{1,3,2,0:T(2,128)}, u32[]{:S(2)}) copy-start(f32[1,256,8,2]{1,3,2,0:T(2,128)} %param.20) | copy-start | bytes 49156
  7.2 13.3 %copy-start.2 = (bf16[1,256,8,128]{3,2,1,0:T(8,128)(2,1)S(1)}, bf16[1,256,8,128]{3,2,1,0:T(8,128)(2,1)}, u32[]{:S(2)}) copy-start(bf16[1,256,8,128]{3,2,1,0:T(8,128)(2,1)} %param.18) | copy-start | bytes 1572868
  7.2 16.7 %copy-start.6 = (f32[8,2]{0,1:T(2,128)S(1)}, f32[8,2]{0,1:T(2,128)}, u32[]{:S(2)}) copy-start(f32[8,2]{0,1:T(2,128)} %param.24) | copy-start | bytes 196
  7.2 74.9 %all-gather.7.cloned.1.call-start = ((), (), s32[]{:S(2)}) async-start(), calls=%async_computation.5 | async-start | bytes 8912896 | tf_op jit(solution)/shard_map/all_gather | solution.py:13
  18.0 124.2 %all-gather.5.cloned.1.call-start = ((), (), s32[]{:S(2)}) async-start(), calls=%async_computation.4 | async-start | bytes 8912896 | tf_op jit(solution)/shard_map/all_gather | solution.py:13
  21.7 528.9 %reduce-scatter.5.cloned.1.call-start = ((), (), s32[]{:S(2)}) async-start(), calls=%async_computation.3 | async-start | bytes 1310720 | tf_op jit(solution)/shard_map/reduce_scatter | solution.py:184
  82.1 81.6 %copy-start.3 = (f32[8,2]{0,1:T(2,128)S(1)}, f32[8,2]{0,1:T(2,128)}, u32[]{:S(2)}) copy-start(f32[8,2]{0,1:T(2,128)} %param.23) | copy-start | bytes 196
  168.5 8.8 %copy-start.1 = (f32[2,1,128,8,2,64]{2,5,4,3,1,0:T(8,128)S(1)}, f32[2,1,128,8,2,64]{2,5,4,3,1,0:T(8,128)}, u32[]{:S(2)}) copy-start(f32[2,1,128,8,2,64]{2,5,4,3,1,0:T(8,128)} %get-tuple-element.1742) | copy-start | bytes 3145732 | tf_op jit(solution)/shard_map/jvp()/while
  183.7 8.8 %copy-start.1 = (f32[2,1,128,8,2,64]{2,5,4,3,1,0:T(8,128)S(1)}, f32[2,1,128,8,2,64]{2,5,4,3,1,0:T(8,128)}, u32[]{:S(2)}) copy-start(f32[2,1,128,8,2,64]{2,5,4,3,1,0:T(8,128)} %get-tuple-element.1742) | copy-start | bytes 3145732 | tf_op jit(solution)/shard_map/jvp()/while
  202.4 12.1 %copy-start = (f32[1,8,2,64,128]{4,3,2,1,0:T(8,128)}, f32[1,8,2,64,128]{4,3,2,1,0:T(8,128)S(1)}, u32[]{:S(2)}) copy-start(f32[1,8,2,64,128]{4,3,2,1,0:T(8,128)S(1)} %dynamic-slice_bitcast_fusion.17) | copy-start | bytes 1572868 | tf_op jit(solution)/shard_map/transpose(jvp())/while
  206.7 15.4 %copy-start.5 = (pred[128]{0:T(512)(128)(4,1)}, pred[128]{0:T(512)(128)(4,1)S(1)}, u32[]{:S(2)}) copy-start(pred[128]{0:T(512)(128)(4,1)S(1)} %broadcast_compare_fusion.5) | copy-start | bytes 388 | tf_op jit(solution)/shard_map/transpose(jvp())/while
  247.2 12.8 %copy-start = (f32[1,8,2,64,128]{4,3,2,1,0:T(8,128)}, f32[1,8,2,64,128]{4,3,2,1,0:T(8,128)S(1)}, u32[]{:S(2)}) copy-start(f32[1,8,2,64,128]{4,3,2,1,0:T(8,128)S(1)} %dynamic-slice_bitcast_fusion.17) | copy-start | bytes 1572868 | tf_op jit(solution)/shard_map/transpose(jvp())/while
  252.1 15.4 %copy-start.5 = (pred[128]{0:T(512)(128)(4,1)}, pred[128]{0:T(512)(128)(4,1)S(1)}, u32[]{:S(2)}) copy-start(pred[128]{0:T(512)(128)(4,1)S(1)} %broadcast_compare_fusion.5) | copy-start | bytes 388 | tf_op jit(solution)/shard_map/transpose(jvp())/while
  288.6 263.7 %reduce-scatter.3.cloned.1.call-start = ((), (), s32[]{:S(2)}) async-start(), calls=%async_computation.2 | async-start | bytes 1310720 | tf_op jit(solution)/shard_map/reduce_scatter | solution.py:183
Sparse Core Ops, SparseCore 0:
  18.1 63.9 all-gather.6
  84.8 57.2 all-gather.4
  288.7 24.6 reduce-scatter.4
  316.2 28.8 reduce-scatter.2
where the time goes:
time: 565 us; the launch traced here: 561 us
  blocking collectives  275 us (49%)
  local copies, waits for them, and re-layouts  81.3 us (14%)
  other arithmetic  75.2 us (13%)
  waiting for transfers between devices  68.2 us (12%)
  matrix products  44.3 us (8%)
  between operations  15.3 us (3%)
    psum x1, blocking collectives, local(): lax.psum((rate_grad, bias_grad, gain_grad), ('seq', 'dp'))  251 us
    all_gather x2, waiting for transfers between devices, prefix(): everything = jax.tree.map(lambda part: lax.all_gather(part, axis), shard)  67.6 us
    select_n x32, other arithmetic, step(): return jax.tree.map(lambda a, b: jnp.where(reached, a, b), new, before)  37.5 us
    all_gather x1, blocking collectives, prefix(): everything = jax.tree.map(lambda part: lax.all_gather(part, axis), shard)  23.6 us
    unnamed x21, local copies, waits for them, and re-layouts  17.9 us
    dot_general x6, matrix products, block_forward(): jnp.einsum('rtsgh,rsghp->rtghp', mixing, head_vals, precision=triple)  14 us
  transfers between devices with their start and end apart: 4, of which 2 were waited for; matrix products, arithmetic and copies ran while one was open for 8% of the time, Pallas kernels for 0%

commit v1 on v0

--- a/solution.py
+++ b/solution.py
@@ -183,7 +183,9 @@
         lax.psum_scatter(keys_grad, "mp", scatter_dimension=2, tiled=True),
         lax.psum_scatter(queries_grad, "mp", scatter_dimension=2, tiled=True),
     )
-    rate_total, bias_total, gain_total = lax.psum((rate_grad, bias_grad, gain_grad), ("seq", "dp"))
+    rate_total, bias_total, gain_total = lax.psum(
+        lax.psum((rate_grad, bias_grad, gain_grad), "seq"), "dp"
+    )
     return (
         mixed_vals.reshape(features.shape).astype(jnp.bfloat16),
         vals_grad.reshape(features.shape).astype(jnp.bfloat16),

time: 565 us -> 360 us (0.64)
  the two profiles are of different devices: /device:TPU:2 before, /device:TPU:8 now
where the time goes in v1:
time: 360 us; the launch traced here: 356 us
  local copies, waits for them, and re-layouts  81.3 us (23%)
  other arithmetic  75.2 us (21%)
  waiting for transfers between devices  72.6 us (20%)
  blocking collectives  65.1 us (18%)
  matrix products  44.3 us (12%)
  between operations  15.3 us (4%)
    all_gather x2, waiting for transfers between devices, prefix(): everything = jax.tree.map(lambda part: lax.all_gather(part, axis), shard)  67.5 us
    select_n x32, other arithmetic, step(): return jax.tree.map(lambda a, b: jnp.where(reached, a, b), new, before)  37.5 us
    psum x1, blocking collectives, local(): lax.psum((rate_grad, bias_grad, gain_grad), 'seq')  25.3 us
    all_gather x1, blocking collectives, prefix(): everything = jax.tree.map(lambda part: lax.all_gather(part, axis), shard)  23.6 us
    unnamed x23, local copies, waits for them, and re-layouts  17.9 us
    psum x1, blocking collectives, local(): lax.psum(lax.psum((rate_grad, bias_grad, gain_grad), 'seq'), 'dp')  16.2 us
    dot_general x6, matrix products, block_forward(): jnp.einsum('rtsgh,rsghp->rtghp', mixing, head_vals, precision=triple)  14 us
    dot_general x8, matrix products, block_forward(): jnp.einsum('rtgn,rsgn->rtsg', query_vals, key_vals, precision=triple)  10.4 us
  transfers between devices with their start and end apart: 4, of which 3 were waited for; matrix products, arithmetic and copies ran while one was open for 12% of the time, Pallas kernels for 0%

profile of v1, /device:TPU:8, one launch (start us, length us, event | category | flops | bytes accessed | tf_op | source)
XLA Modules:
  0.0 355.7 jit_solution(3272531039260423616)
XLA Ops:
  15.7 2.3 fusion.127
  19.0 1.3 copy.464
  21.8 1.5 reshape.1086
  24.7 2.1 copy.470
  26.8 2.1 copy.469
  30.1 23.6 %all_gather.18 = f32[16,1,8,2]{2,3,1,0:T(2,128)S(1)} all-gather(f32[1,1,8,2]{2,3,1,0:T(2,128)S(1)} %copy.462), channel_id=1, replica_groups=mesh['seq'=16,'dp'=8,'mp'=4] {'seq'}, dimensions={0}, use_global_device_ids=true | all-gather | bytes 1088 | tf_op jit(solution)/shard_map/all_gather | solution.py:13
  53.7 28.3 %all-gather.7.cloned.1.call-done = f32[128,2,64,128]{3,2,1,0:T(8,128)} async-done(((f32[8,2,64,128]{3,2,1,0:T(8,128)}), f32[128,2,64,128]{3,2,1,0:T(8,128)}) %all-gather.7.cloned.1.call-update) | async-done | bytes 8388624 | tf_op jit(solution)/shard_map/all_gather | solution.py:13
  82.0 20.8 %while.78 = (s32[]{:T(128)}, f32[1,8,2,64,128]{4,3,2,1,0:T(8,128)S(1)}, s32[]{:T(128)}, f32[16,1,8,2,64,128]{5,4,3,2,1,0:T(8,128)}, f32[16,1,8,2]{2,3,1,0:T(2,12...) while((s32[]{:T(128)}, f32[1,8,2,64,128]{4,3,2,1,0:T(8,128)S(1)}, s32[]{:T(128)}, ...), condition=%wide.region_11.12_spmd.clone, body=%wide.region_10.11_spmd.clone.sunk | while | flops 524296 | bytes 1573359 | solution.py:26
  102.9 39.2 %all-gather.5.cloned.1.call-done = f32[128,2,64,128]{3,2,1,0:T(8,128)} async-done(((f32[8,2,64,128]{3,2,1,0:T(8,128)}), f32[128,2,64,128]{3,2,1,0:T(8,128)}) %all-gather.5.cloned.1.call-update) | async-done | bytes 8388624 | tf_op jit(solution)/shard_map/all_gather | solution.py:13
  142.0 20.6 %while.77 = (s32[]{:T(128)}, f32[1,8,2,64,128]{4,3,2,1,0:T(8,128)S(1)}, s32[]{:T(128)}, f32[16,1,8,2]{2,3,1,0:T(2,128)S(1)}, f32[16,1,8,2,64,128]{5,4,3,2,1,0:T(8,128)}, /*index=5*/s32[]{:T(128)}, s32[]{:T(128)}) while((s32[]{:T(128)}, f32[1,8,2,64,128]{4,3,2,1,0:T(8,128)S(1)}, s32[]{:T(128)}, f32[16,1,8,2]{2,3,1,0:T(2,128)S(1)}, ...), condition=%wide.region_5.6_spmd.clone, body=%wide.region_4.5_spmd.clone.sunk | while | flops 524292 | bytes 1573297 | solution.py:26
  163.6 30.4 %while.76 = (s32[]{:T(128)}, f32[1,8,2,64,128]{4,3,2,1,0:T(8,128)S(1)}, bf16[2,1,128,8,2,64]{2,5,4,3,1,0:T(8,128)(2,1)}, f32[2,1,8,2,64,128]{5,4,3,2,1,0:T(8,128...) while((s32[]{:T(128)}, ...), condition=%wide.region_9.10_spmd.clone, body=%wide.region_6.9_spmd.clone.sunk | while | flops 405264384 | bytes 14427908 | solution.py:139
  168.4 1.8 fusion.210
  170.3 1.9 convolution_bitcast_fusion.16
  173.1 3.3 fusion.211
  177.2 1.5 fusion.209
  183.6 1.8 fusion.210
  185.4 1.9 convolution_bitcast_fusion.16
  188.3 3.3 fusion.211
  192.4 1.5 fusion.209
  197.8 90.8 %while.79 = (s32[]{:T(128)}, f32[8,2]{1,0:T(8,128)}, f32[8,2]{0,1:T(2,128)}, f32[8,2]{1,0:T(8,128)}, f32[1,8,2,64,128]{4,3,2,1,0:T(8,128)S(1)}, /*index=5*/bf16[...) while((s32[]{:T(128)}, f32[8,2]{1,0:T(8,128)}, ...), condition=%wide.region_25.26_spmd.clone, body=%wide.region_12.25_spmd.clone.sunk | while | flops 1015154816 | bytes 36794436 | solution.py:139
  198.4 1.8 constant_dynamic-slice_fusion.4
  202.4 1.5 dynamic-slice_bitcast_fusion.19
  207.4 1.5 convolution_bitcast_fusion.17
  208.8 2.0 copy.623
  210.8 2.0 copy.612
  212.9 1.5 fusion.234
  220.5 1.6 convolution_bitcast_fusion.19
  223.1 3.3 fusion.239
  229.7 1.9 fusion.242
  235.6 2.7 fusion.245
  238.3 1.4 dynamic_update_slice.74
  243.1 1.8 constant_dynamic-slice_fusion.4
  247.1 1.5 dynamic-slice_bitcast_fusion.19
  252.8 1.5 convolution_bitcast_fusion.17
  254.2 2.0 copy.623
  256.3 2.0 copy.612
  258.3 1.5 fusion.234
  265.9 1.6 convolution_bitcast_fusion.19
  268.5 3.3 fusion.239
  275.1 1.9 fusion.242
  281.7 2.7 fusion.245
  284.4 1.4 dynamic_update_slice.74
  290.7 1.3 transpose.190
  292.0 2.5 copy.509
  295.8 2.5 copy.512
  299.6 25.3 %all-reduce.2 = (f32[8,2]{0,1:T(2,128)S(1)}, f32[8,2]{0,1:T(2,128)S(1)}, f32[8,2]{0,1:T(2,128)S(1)}) all-reduce(f32[8,2]{0,1:T(2,128)S(1)} %copy-done.7, f32[8,2]{0,1:T(2,128)S(1)} %copy.487, f32[8,2]{0,1:T(2,128)S(1)} %copy.488), channel_id=1, replica_groups=mesh['seq'=16,'dp'=8,'mp'=4] {'seq'}, use_global_device_ids=true, to_apply=%region_28.29 | all-reduce | flops 48 | bytes 384 | tf_op jit(solution)/shard_map/psum | solution.py:187
  324.8 16.2 %all-reduce.3 = (f32[8,2]{0,1:T(2,128)}, f32[8,2]{0,1:T(2,128)}, f32[8,2]{0,1:T(2,128)}) all-reduce(f32[8,2]{0,1:T(2,128)S(1)} %get-tuple-element.1337, f32[8,2]{0,1:T(2,128)S(1)} %get-tuple-element.1338, f32[8,2]{0,1:T(2,128)S(1)} %get-tuple-element.1339), channel_id=1, replica_groups=mesh['seq'=16,'dp'=8,'mp'=4] {'dp'}, use_global_device_ids=true, to_apply=%region_29.30 | all-reduce | flops 48 | bytes 384 | tf_op jit(solution)/shard_map/psum | solution.py:186
  342.8 4.5 %reduce-scatter.3.cloned.1.call-done = f32[1,256,2,128]{3,1,0,2:T(8,128)} async-done(((f32[1,256,8,128]{3,1,0,2:T(8,128)}), f32[1,256,2,128]{3,1,0,2:T(8,128)}) %reduce-scatter.3.cloned.1.call-update) | async-done | bytes 262160 | tf_op jit(solution)/shard_map/reduce_scatter | solution.py:183
  (313 shorter events, 126.6 us)
Async XLA Ops:
  7.2 14.6 %copy-start.4 = (f32[1,256,8,2]{1,3,2,0:T(2,128)S(1)}, f32[1,256,8,2]{1,3,2,0:T(2,128)}, u32[]{:S(2)}) copy-start(f32[1,256,8,2]{1,3,2,0:T(2,128)} %param.20) | copy-start | bytes 49156
  7.2 13.3 %copy-start.2 = (bf16[1,256,8,128]{3,2,1,0:T(8,128)(2,1)S(1)}, bf16[1,256,8,128]{3,2,1,0:T(8,128)(2,1)}, u32[]{:S(2)}) copy-start(bf16[1,256,8,128]{3,2,1,0:T(8,128)(2,1)} %param.18) | copy-start | bytes 1572868
  7.2 16.7 %copy-start.6 = (f32[8,2]{0,1:T(2,128)S(1)}, f32[8,2]{0,1:T(2,128)}, u32[]{:S(2)}) copy-start(f32[8,2]{0,1:T(2,128)} %param.24) | copy-start | bytes 196
  7.2 74.8 %all-gather.7.cloned.1.call-start = ((), (), s32[]{:S(2)}) async-start(), calls=%async_computation.5 | async-start | bytes 8912896 | tf_op jit(solution)/shard_map/all_gather | solution.py:13
  18.0 124.1 %all-gather.5.cloned.1.call-start = ((), (), s32[]{:S(2)}) async-start(), calls=%async_computation.4 | async-start | bytes 8912896 | tf_op jit(solution)/shard_map/all_gather | solution.py:13
  21.7 319.4 %reduce-scatter.5.cloned.1.call-start = ((), (), s32[]{:S(2)}) async-start(), calls=%async_computation.3 | async-start | bytes 1310720 | tf_op jit(solution)/shard_map/reduce_scatter | solution.py:184
  82.0 81.6 %copy-start.3 = (f32[8,2]{0,1:T(2,128)S(1)}, f32[8,2]{0,1:T(2,128)}, u32[]{:S(2)}) copy-start(f32[8,2]{0,1:T(2,128)} %param.23) | copy-start | bytes 196
  168.4 8.8 %copy-start.1 = (f32[2,1,128,8,2,64]{2,5,4,3,1,0:T(8,128)S(1)}, f32[2,1,128,8,2,64]{2,5,4,3,1,0:T(8,128)}, u32[]{:S(2)}) copy-start(f32[2,1,128,8,2,64]{2,5,4,3,1,0:T(8,128)} %get-tuple-element.1745) | copy-start | bytes 3145732 | tf_op jit(solution)/shard_map/jvp()/while
  183.6 8.8 %copy-start.1 = (f32[2,1,128,8,2,64]{2,5,4,3,1,0:T(8,128)S(1)}, f32[2,1,128,8,2,64]{2,5,4,3,1,0:T(8,128)}, u32[]{:S(2)}) copy-start(f32[2,1,128,8,2,64]{2,5,4,3,1,0:T(8,128)} %get-tuple-element.1745) | copy-start | bytes 3145732 | tf_op jit(solution)/shard_map/jvp()/while
  202.4 12.1 %copy-start = (f32[1,8,2,64,128]{4,3,2,1,0:T(8,128)}, f32[1,8,2,64,128]{4,3,2,1,0:T(8,128)S(1)}, u32[]{:S(2)}) copy-start(f32[1,8,2,64,128]{4,3,2,1,0:T(8,128)S(1)} %dynamic-slice_bitcast_fusion.17) | copy-start | bytes 1572868 | tf_op jit(solution)/shard_map/transpose(jvp())/while
  206.7 15.4 %copy-start.5 = (pred[128]{0:T(512)(128)(4,1)}, pred[128]{0:T(512)(128)(4,1)S(1)}, u32[]{:S(2)}) copy-start(pred[128]{0:T(512)(128)(4,1)S(1)} %broadcast_compare_fusion.5) | copy-start | bytes 388 | tf_op jit(solution)/shard_map/transpose(jvp())/while
  247.1 12.8 %copy-start = (f32[1,8,2,64,128]{4,3,2,1,0:T(8,128)}, f32[1,8,2,64,128]{4,3,2,1,0:T(8,128)S(1)}, u32[]{:S(2)}) copy-start(f32[1,8,2,64,128]{4,3,2,1,0:T(8,128)S(1)} %dynamic-slice_bitcast_fusion.17) | copy-start | bytes 1572868 | tf_op jit(solution)/shard_map/transpose(jvp())/while
  252.1 15.4 %copy-start.5 = (pred[128]{0:T(512)(128)(4,1)}, pred[128]{0:T(512)(128)(4,1)S(1)}, u32[]{:S(2)}) copy-start(pred[128]{0:T(512)(128)(4,1)S(1)} %broadcast_compare_fusion.5) | copy-start | bytes 388 | tf_op jit(solution)/shard_map/transpose(jvp())/while
  288.5 11.0 %copy-start.7 = (f32[8,2]{0,1:T(2,128)S(1)}, f32[8,2]{0,1:T(2,128)}, u32[]{:S(2)}) copy-start(f32[8,2]{0,1:T(2,128)} %get-tuple-element.780) | copy-start | bytes 196
  288.6 58.8 %reduce-scatter.3.cloned.1.call-start = ((), (), s32[]{:S(2)}) async-start(), calls=%async_computation.2 | async-start | bytes 1310720 | tf_op jit(solution)/shard_map/reduce_scatter | solution.py:183
Sparse Core Ops, SparseCore 0:
  18.1 63.9 all-gather.6
  84.7 57.2 all-gather.4
  288.7 27.1 reduce-scatter.4
  318.6 28.7 reduce-scatter.2
